TPU v7x, 32 devices: a whole 2x2x4 slice. The times are simulated.
32 devices in a mesh: band: 16 (over z, y, x), mem: 2 (over core).
Axes of the slice: x: 2, y: 2, z: 4, core: 2. Of those that a mesh axis runs over, the one named last changes fastest.
Arguments:
- state: float32 [16384, 2048], P('band', 'mem'), may hold values from -10 to 10
- obs_anom: bfloat16 [4096, 2048], P('band', 'mem'), may hold values from -8 to 8
- innov: float32 [4096, 2048], P('band', 'mem'), may hold values from -12 to 12
- pattern: int32 [16, 4, 8, 4], P('band'), may hold values 0 or 1
- distance: int32 [16, 4, 8, 4], P('band'), may hold values from 0 to 7
- taper: float32 [8], replicated, may hold values from 0.2 to 1
- order: int32 [16, 4], P('band'), may hold values from 0 to 3, each once within a row
Outputs:
- analysis: float32 [16384, 2048], P('band', 'mem')
Inputs may be any that keep to these rules, and one draw needn't show every extreme that they name: Each row of order lists 0 .. 3 once each.
All inputs are finite; a program needn't handle non-finite values. No bound on the sum of `pattern` on one device may be relied on, other than what follows from the above.
Results may differ from a plain program's by a relative error of at most 0.0028.
Values may be sent and summed in bfloat16 or wider, within the bound.
A program may use at most 64 MiB of HBM per device.

v0:
```python
import jax
import jax.numpy as jnp
from jax import lax
from jax.sharding import PartitionSpec as P


def from_behind(value, axis, steps):
    count = lax.axis_size(axis)
    pairs = [(source, (source + steps) % count) for source in range(count)]
    return lax.ppermute(value, axis, pairs)


def spread(blocks):
    rows, cols = blocks.shape
    return jnp.broadcast_to(blocks[:, None, :, None], (rows, 128, cols, 64)).reshape(
        rows * 128, cols * 64
    )


def on_device(state, obs_anom, innov, pattern, distance, taper, order):
    members = lax.axis_size("mem") * state.shape[1]
    scale = 1.0 / (members - 1)
    num_obs = obs_anom.shape[0]
    arrivals = order.shape[1]
    gram_part = jnp.dot(obs_anom, obs_anom.T, preferred_element_type=jnp.float32)
    gram = lax.psum(gram_part, "mem")
    spd = gram * scale + jnp.eye(num_obs, dtype=jnp.float32)
    factor = jnp.linalg.cholesky(spd)
    weights_own = jax.scipy.linalg.cho_solve((factor, True), innov).astype(jnp.bfloat16)
    own_batch = jnp.stack([obs_anom, weights_own])
    batches = [own_batch]
    current = own_batch
    for offset in range(1, arrivals):
        current = from_behind(current, "band", 1)
        batches.append(current)
    stacked = jnp.stack(batches)
    onehot = (distance[0][..., None] == jnp.arange(taper.shape[0], dtype=jnp.int32)).astype(
        jnp.float32
    )
    local = pattern[0].astype(jnp.float32) * jnp.sum(onehot * taper, axis=-1)
    field = state
    for step in range(arrivals):
        offset = order[0, step]
        chosen = lax.dynamic_index_in_dim(stacked, offset, 0, keepdims=False)
        y_batch = chosen[0].astype(jnp.float32)
        w_batch = chosen[1].astype(jnp.float32)
        blocks = lax.dynamic_index_in_dim(local, offset, 0, keepdims=False)
        cross_part = jnp.dot(field, y_batch.T, precision=lax.Precision.HIGHEST)
        cross = lax.psum(cross_part, "mem")
        field = field + jnp.dot(
            cross * scale * spread(blocks), w_batch, precision=lax.Precision.HIGHEST
        )
    return field


def solution(mesh):
    return jax.shard_map(
        on_device,
        mesh=mesh,
        in_specs=(
            P("band", "mem"),
            P("band", "mem"),
            P("band", "mem"),
            P("band", None, None, None),
            P("band", None, None, None),
            P(),
            P("band", None),
        ),
        out_specs=P("band", "mem"),
        check_vma=False,
    )
```

profile of v0, /device:TPU:0, one launch (start us, length us, event | category | flops | bytes accessed | tf_op | source)
XLA Modules:
  0.0 313.7 jit_solution(5123660919342085485)
XLA Ops:
  6.5 2.3 fusion.45
  9.0 21.7 %all-reduce.7.cloned.1.call-done = f32[256,256]{0,1:T(8,128)} async-done(((f32[256,256]{0,1:T(8,128)}), f32[256,256]{0,1:T(8,128)}) %all-reduce.7.cloned.1.call-update) | async-done | bytes 262160 | tf_op jit(solution)/shard_map/psum | solution.py:26
  30.6 1.0 convert_add_fusion
  31.8 1.0 fusion.18
  32.8 11.7 %cholesky.50 = f32[128,128]{1,0:T(8,128)S(1)} custom-call(f32[128,128]{1,0:T(8,128)S(1)} %cholesky.118), custom_call_target="Cholesky" | custom-call | tf_op jit(solution)/shard_map/jit(cholesky)/cholesky | solution.py:28
  44.5 9.8 %custom-call.18 = f32[1,128,128]{1,2,0:T(8,128)S(1)} custom-call(f32[1,128,128]{2,1,0:T(8,128)S(1)} %get-tuple-element.28), custom_call_target="InvertDiagBlocksLowerTriangular" | custom-call | tf_op jit(solution)/shard_map/jit(cholesky)/cholesky | solution.py:28
  54.9 11.7 %cholesky.105 = f32[128,128]{1,0:T(8,128)S(1)} custom-call(f32[128,128]{1,0:T(8,128)S(1)} %convolution_subtract_fusion.2), custom_call_target="Cholesky" | custom-call | tf_op jit(solution)/shard_map/jit(cholesky)/cholesky | solution.py:28
  68.8 4.2 %while.1 = (s32[]{:T(128)}, f32[256,256]{1,0:T(8,128)S(1)}, s32[2,2]{1,0:T(2,128)S(1)}, f32[2,128,128]{2,1,0:T(8,128)S(1)}, s32[]{:T(128)}) while((s32[]{:T(128)}, f32[256,256]{1,0:T(8,128)S(1)}, s32[2,2]{1,0:T(2,128)S(1)}, f32[2,128,128]{2,1,0:T(8,128)S(1)}, s32[]{:T(128)}) %tuple.30), condition=%wide.while_cond, body=%wide.while_body.sunk | while | flops 2 | bytes 131181 | solution.py:29
  69.5 1.4 bitcast_dynamic-update-slice_fusion.2
  71.5 1.4 bitcast_dynamic-update-slice_fusion.2
  73.0 19.7 %custom-call.19 = f32[2,128,128]{1,2,0:T(8,128)S(1)} custom-call(f32[2,128,128]{2,1,0:T(8,128)S(1)} %get-tuple-element.12), custom_call_target="InvertDiagBlocksLowerTriangular" | custom-call | tf_op jit(solution)/shard_map/jit(_cho_solve)/triangular_solve | solution.py:29
  96.6 1.8 collective-permute-start
  98.4 27.3 %collective-permute-done = bf16[2,256,1024]{2,1,0:T(8,128)(2,1)S(1)} collective-permute-done((bf16[2,256,1024]{2,1,0:T(8,128)(2,1)S(1)}, bf16[2,256,1024]{2,1,0:T(8,128)(2,1)S(1)}, u32[]{:S(2)}, u32[]{:S(2)}) %collective-permute-start) | collective-permute-done | bytes 1048608 | tf_op jit(solution)/shard_map/ppermute | solution.py:10
  125.7 28.3 %collective-permute-done.1 = bf16[2,256,1024]{2,1,0:T(8,128)(2,1)} collective-permute-done((bf16[2,256,1024]{2,1,0:T(8,128)(2,1)S(1)}, bf16[2,256,1024]{2,1,0:T(8,128)(2,1)}, u32[]{:S(2)}, u32[]{:S(2)}) %collective-permute-start.1) | collective-permute-done | bytes 1048608 | tf_op jit(solution)/shard_map/ppermute | solution.py:10
  156.6 25.0 %collective-permute-done.2 = bf16[2,256,1024]{2,1,0:T(8,128)(2,1)} collective-permute-done((bf16[2,256,1024]{2,1,0:T(8,128)(2,1)}, bf16[2,256,1024]{2,1,0:T(8,128)(2,1)}, u32[]{:S(2)}, u32[]{:S(2)}) %collective-permute-start.2) | collective-permute-done | bytes 1048608 | tf_op jit(solution)/shard_map/ppermute | solution.py:10
  181.6 1.9 pad_maximum_fusion
  183.5 1.9 copy-done.3
  185.5 3.2 %convolution_bitcast_fusion = f32[1024,256]{0,1:T(8,128)} fusion(f32[1024,1024]{1,0:T(8,128)S(1)} %copy-done.4, bf16[4,2,256,1024]{3,2,1,0:T(8,128)(2,1)S(1)} %pad_maximum_fusion, s32[]{:T(128)S(6)} %select_n.23), kind=kOutput, calls=%fused_computation.7 | convolution fusion | flops 3221225472 | bytes 5767172 | tf_op jit(solution)/shard_map/dot_general | solution.py:48
  195.0 9.1 %all-reduce.9.cloned.1.call-done = f32[1024,256]{0,1:T(8,128)} async-done(((f32[1024,256]{0,1:T(8,128)}), f32[1024,256]{0,1:T(8,128)}) %all-reduce.9.cloned.1.call-update) | async-done | bytes 1048592 | tf_op jit(solution)/shard_map/psum | solution.py:49
  204.2 4.9 %convolution_add_fusion.3 = f32[1024,1024]{1,0:T(8,128)S(1)} fusion(f32[1024,1024]{1,0:T(8,128)} %param.7, f32[32,8,8,128]{3,2,1,0:T(8,128)S(1)} %bitcast.125, f32[1024,256]{0,1:T(8,128)} %all-reduce.9.cloned.1.call-done, bf16[4,2,256,1024]{3,2,1,0:T(8,128)(2,1)} %copy-done.3, s32[]{:T(128)S(6)} %select_n.23, s32[]{:T(128)S(6)} %add.80), kind=kOutput, calls=%fused_computation.6 | convolution fusion | flops 3222798336 | bytes 11010056 | tf_op jit(solution)/shard_map/dot_general | solution.py:50
  209.1 2.0 copy-done.2
  211.1 4.2 %fusion.11 = f32[1024,256]{0,1:T(8,128)} fusion(f32[1024,1024]{1,0:T(8,128)S(1)} %convolution_add_fusion.3, bf16[4,2,256,1024]{3,2,1,0:T(8,128)(2,1)} %copy-done.3, s32[]{:T(128)S(6)} %select_n.24), kind=kOutput, calls=%fused_computation.34 | convolution fusion | flops 3221225472 | bytes 5767172 | tf_op jit(solution)/shard_map/dot_general | solution.py:48
  215.5 20.7 %all-reduce.11.cloned.1.call-done = f32[1024,256]{0,1:T(8,128)} async-done(((f32[1024,256]{0,1:T(8,128)}), f32[1024,256]{0,1:T(8,128)}) %all-reduce.11.cloned.1.call-update) | async-done | bytes 1048592 | tf_op jit(solution)/shard_map/psum | solution.py:49
  236.3 4.9 %convolution_add_fusion.2 = f32[1024,1024]{1,0:T(8,128)S(1)} fusion(f32[1024,1024]{1,0:T(8,128)} %copy-done.2, f32[32,8,8,128]{3,2,1,0:T(8,128)S(1)} %bitcast.123, f32[1024,256]{0,1:T(8,128)} %all-reduce.11.cloned.1.call-done, bf16[4,2,256,1024]{3,2,1,0:T(8,128)(2,1)} %copy-done.3, s32[]{:T(128)S(6)} %select_n.24, s32[]{:T(128)S(6)} %add.80), kind=kOutput, calls=%fused_computation.5 | convolution fusion | flops 3222798336 | bytes 11010056 | tf_op jit(solution)/shard_map/dot_general | solution.py:50
  241.2 2.0 copy-done.1
  243.2 4.2 %fusion.10 = f32[1024,256]{0,1:T(8,128)} fusion(f32[1024,1024]{1,0:T(8,128)S(1)} %convolution_add_fusion.2, bf16[4,2,256,1024]{3,2,1,0:T(8,128)(2,1)} %copy-done.3, s32[]{:T(128)S(6)} %select_n.25), kind=kOutput, calls=%fused_computation.31 | convolution fusion | flops 3221225472 | bytes 5767172 | tf_op jit(solution)/shard_map/dot_general | solution.py:48
  247.8 20.5 %all-reduce.13.cloned.1.call-done = f32[1024,256]{0,1:T(8,128)} async-done(((f32[1024,256]{0,1:T(8,128)}), f32[1024,256]{0,1:T(8,128)}) %all-reduce.13.cloned.1.call-update) | async-done | bytes 1048592 | tf_op jit(solution)/shard_map/psum | solution.py:49
  268.4 4.9 %convolution_add_fusion.1 = f32[1024,1024]{1,0:T(8,128)S(1)} fusion(f32[1024,1024]{1,0:T(8,128)} %copy-done.1, f32[32,8,8,128]{3,2,1,0:T(8,128)S(1)} %bitcast.124, f32[1024,256]{0,1:T(8,128)} %all-reduce.13.cloned.1.call-done, bf16[4,2,256,1024]{3,2,1,0:T(8,128)(2,1)} %copy-done.3, s32[]{:T(128)S(6)} %select_n.25, s32[]{:T(128)S(6)} %add.80), kind=kOutput, calls=%fused_computation.4 | convolution fusion | flops 3222798336 | bytes 11010056 | tf_op jit(solution)/shard_map/dot_general | solution.py:50
  273.3 2.0 copy-done
  275.3 4.3 %fusion.9 = f32[1024,256]{0,1:T(8,128)} fusion(f32[1024,1024]{1,0:T(8,128)S(1)} %convolution_add_fusion.1, bf16[4,2,256,1024]{3,2,1,0:T(8,128)(2,1)} %copy-done.3, s32[]{:T(128)S(6)} %select_n.26), kind=kOutput, calls=%fused_computation.28 | convolution fusion | flops 3221225472 | bytes 5767172 | tf_op jit(solution)/shard_map/dot_general | solution.py:48
  279.6 20.8 %all-reduce.15.cloned.1.call-done = f32[1024,256]{0,1:T(8,128)} async-done(((f32[1024,256]{0,1:T(8,128)}), f32[1024,256]{0,1:T(8,128)}) %all-reduce.15.cloned.1.call-update) | async-done | bytes 1048592 | tf_op jit(solution)/shard_map/psum | solution.py:49
  300.5 6.7 %convolution_add_fusion = f32[1024,1024]{1,0:T(8,128)} fusion(f32[1024,1024]{1,0:T(8,128)} %copy-done, f32[32,8,8,128]{3,2,1,0:T(8,128)S(1)} %bitcast.122, f32[1024,256]{0,1:T(8,128)} %all-reduce.15.cloned.1.call-done, bf16[4,2,256,1024]{3,2,1,0:T(8,128)(2,1)} %copy-done.3, s32[]{:T(128)S(6)} %select_n.26, s32[]{:T(128)S(6)} %add.80), kind=kOutput, calls=%fused_computation.3 | convolution fusion | flops 3222798336 | bytes 11010056 | tf_op jit(solution)/shard_map/dot_general | solution.py:50
  (62 shorter events, 8.7 us)
Async XLA Ops:
  6.5 86.1 %copy-start.6 = (f32[256,1024]{1,0:T(8,128)S(1)}, f32[256,1024]{1,0:T(8,128)}, u32[]{:S(2)}) copy-start(f32[256,1024]{1,0:T(8,128)} %param.9) | copy-start | bytes 3145732
  6.5 24.1 %all-reduce.7.cloned.1.call-start = ((), (), s32[]{:S(2)}) async-start(), calls=%async_computation | async-start | bytes 524288 | tf_op jit(solution)/shard_map/psum | solution.py:26
  8.9 195.2 %all-reduce.9.cloned.1.call-start = ((), (), s32[]{:S(2)}) async-start(), calls=%async_computation.1 | async-start | bytes 2097152 | tf_op jit(solution)/shard_map/psum | solution.py:49
  73.0 23.4 %copy-start.5 = (bf16[256,1024]{1,0:T(8,128)(2,1)S(1)}, bf16[256,1024]{1,0:T(8,128)(2,1)}, u32[]{:S(2)}) copy-start(bf16[256,1024]{1,0:T(8,128)(2,1)} %param.8) | copy-start | bytes 1572868
  93.9 60.0 %copy-start.9 = (s32[1,4]{1,0:T(1,128)S(1)}, s32[1,4]{1,0:T(1,128)}, u32[]{:S(2)}) copy-start(s32[1,4]{1,0:T(1,128)} %param.13) | copy-start | bytes 52
  96.6 29.1 %collective-permute-start = (bf16[2,256,1024]{2,1,0:T(8,128)(2,1)S(1)}, bf16[2,256,1024]{2,1,0:T(8,128)(2,1)S(1)}, u32[]{:S(2)}, u32[]{:S(2)}) collective-permute-start(bf16[2,256,1024]{2,1,0:T(8,128)(2,1)S(1)} %get-tuple-element.24), channel_id=1, source_target_pairs={{0,2},{2,4},{4,6},{6,8},{8,10},{10,12},{12,14},{14,16},{16,18},{18... | collective-permute-start | bytes 3145736 | tf_op jit(solution)/shard_map/ppermute | solution.py:10
  125.7 28.3 %collective-permute-start.1 = (bf16[2,256,1024]{2,1,0:T(8,128)(2,1)S(1)}, bf16[2,256,1024]{2,1,0:T(8,128)(2,1)}, u32[]{:S(2)}, u32[]{:S(2)}) collective-permute-start(bf16[2,256,1024]{2,1,0:T(8,128)(2,1)S(1)} %collective-permute-done), channel_id=1, source_target_pairs={{0,2},{2,4},{4,6},{6,8},{8,10},{10,12},{12,14},{14,16},{16,18},{18... | collective-permute-start | bytes 3145736 | tf_op jit(solution)/shard_map/ppermute | solution.py:10
  153.9 27.6 %collective-permute-start.2 = (bf16[2,256,1024]{2,1,0:T(8,128)(2,1)}, bf16[2,256,1024]{2,1,0:T(8,128)(2,1)}, u32[]{:S(2)}, u32[]{:S(2)}) collective-permute-start(bf16[2,256,1024]{2,1,0:T(8,128)(2,1)} %collective-permute-done.1), channel_id=1, source_target_pairs={{0,2},{2,4},{4,6},{6,8},{8,10},{10,12},{12,14},{14,16},{16,18},{18... | collective-permute-start | bytes 3145736 | tf_op jit(solution)/shard_map/ppermute | solution.py:10
  181.6 3.9 %copy-start.4 = (f32[1024,1024]{1,0:T(8,128)S(1)}, f32[1024,1024]{1,0:T(8,128)}, u32[]{:S(2)}) copy-start(f32[1024,1024]{1,0:T(8,128)} %param.7) | copy-start | bytes 12582916
  183.5 1.9 copy-start.3
  185.4 9.3 %copy-start.8 = (s32[1,4,8,4]{2,3,1,0:T(4,128)S(1)}, s32[1,4,8,4]{2,3,1,0:T(4,128)}, u32[]{:S(2)}) copy-start(s32[1,4,8,4]{2,3,1,0:T(4,128)} %param.11) | copy-start | bytes 1540
  185.4 9.3 %copy-start.10 = (f32[8]{0:T(128)S(1)}, f32[8]{0:T(128)}, u32[]{:S(2)}) copy-start(f32[8]{0:T(128)} %param.12) | copy-start | bytes 100
  185.5 9.5 %copy-start.7 = (s32[1,4,8,4]{2,3,1,0:T(4,128)S(1)}, s32[1,4,8,4]{2,3,1,0:T(4,128)}, u32[]{:S(2)}) copy-start(s32[1,4,8,4]{2,3,1,0:T(4,128)} %param.10) | copy-start | bytes 1540
  188.6 47.5 %all-reduce.11.cloned.1.call-start = ((), (), s32[]{:S(2)}) async-start(), calls=%async_computation.2 | async-start | bytes 2097152 | tf_op jit(solution)/shard_map/psum | solution.py:49
  209.1 2.0 copy-start.2
  215.4 52.9 %all-reduce.13.cloned.1.call-start = ((), (), s32[]{:S(2)}) async-start(), calls=%async_computation.3 | async-start | bytes 2097152 | tf_op jit(solution)/shard_map/psum | solution.py:49
  241.2 2.0 copy-start.1
  247.5 52.9 %all-reduce.15.cloned.1.call-start = ((), (), s32[]{:S(2)}) async-start(), calls=%async_computation.4 | async-start | bytes 2097152 | tf_op jit(solution)/shard_map/psum | solution.py:49
  273.3 2.0 copy-start
Sparse Core Ops, SparseCore 0:
  9.7 20.9 all-reduce.6
  188.8 15.2 all-reduce.8
  215.5 20.5 all-reduce.10
  247.6 20.6 all-reduce.12
  279.7 20.5 all-reduce.14
where the time goes:
time: 314 us
  waiting for transfers between devices  173 us (55%)
  other arithmetic  58 us (18%)
  matrix products  43.7 us (14%)
  between operations  22.5 us (7%)
  local copies, waits for them, and re-layouts  13.5 us (4%)
    ppermute x3, waiting for transfers between devices, from_behind(): return lax.ppermute(value, axis, pairs)  80.5 us
    psum x4, waiting for transfers between devices, on_device(): cross = lax.psum(cross_part, 'mem')  71 us
    another operation x6, other arithmetic, on_device(): factor = jnp.linalg.cholesky(spd)  34 us
    psum x1, waiting for transfers between devices, on_device(): gram = lax.psum(gram_part, 'mem')  21.7 us
    dot_general x4, matrix products, on_device(): jnp.dot(cross * scale * spread(blocks), w_batch, precision=lax.Precision....  21.4 us
    another operation x4, other arithmetic, on_device(): jax.scipy.linalg.cho_solve((factor, True), innov).astype(jnp.bfloat16)  19.7 us
    dot_general x4, matrix products, on_device(): cross_part = jnp.dot(field, y_batch.T, precision=lax.Precision.HIGHEST)  15.9 us
    unnamed x22, local copies, waits for them, and re-layouts  7.98 us
  transfers between devices with their start and end apart: 8, of which 8 were waited for; matrix products, arithmetic and copies ran while one was open for 0% of the time, Pallas kernels for 0%

commit v1 on v0

--- a/solution.py
+++ b/solution.py
@@ -23,7 +23,8 @@
     num_obs = obs_anom.shape[0]
     arrivals = order.shape[1]
     gram_part = jnp.dot(obs_anom, obs_anom.T, preferred_element_type=jnp.float32)
-    gram = lax.psum(gram_part, "mem")
+    pieces = lax.all_gather(gram_part, "mem")
+    gram = jnp.sum(pieces, axis=0)
     spd = gram * scale + jnp.eye(num_obs, dtype=jnp.float32)
     factor = jnp.linalg.cholesky(spd)
     weights_own = jax.scipy.linalg.cho_solve((factor, True), innov).astype(jnp.bfloat16)

time: 314 us -> 294 us (0.936)
  waiting for transfers between devices: 173 us -> 152 us
    psum x1 -> x0, waiting for transfers between devices: 21.7 us -> none  [on_device(): gram = lax.psum(gram_part, 'mem')]
  transfers between devices with their start and end apart: 8 -> 7, of which waited for: 8 -> 7; matrix products, arithmetic and copies ran while one was open for 0% -> 0% of each run, Pallas kernels for 0% -> 0%
where the time goes in v1:
time: 294 us; the launch traced here: 293 us
  waiting for transfers between devices  152 us (52%)
  other arithmetic  56.2 us (19%)
  matrix products  43 us (15%)
  between operations  22.2 us (8%)
  local copies, waits for them, and re-layouts  13.4 us (5%)
  starting transfers between devices  3.51 us (1%)
    ppermute x3, waiting for transfers between devices, from_behind(): return lax.ppermute(value, axis, pairs)  80.8 us
    psum x4, waiting for transfers between devices, on_device(): cross = lax.psum(cross_part, 'mem')  71.4 us
    another operation x6, other arithmetic, on_device(): factor = jnp.linalg.cholesky(spd)  34 us
    dot_general x4, matrix products, on_device(): jnp.dot(cross * scale * spread(blocks), w_batch, precision=lax.Precision....  21.4 us
    another operation x4, other arithmetic, on_device(): jax.scipy.linalg.cho_solve((factor, True), innov).astype(jnp.bfloat16)  19.7 us
    dot_general x4, matrix products, on_device(): cross_part = jnp.dot(field, y_batch.T, precision=lax.Precision.HIGHEST)  15.9 us
    unnamed x22, local copies, waits for them, and re-layouts  7.98 us
  transfers between devices with their start and end apart: 7, of which 7 were waited for; matrix products, arithmetic and copies ran while one was open for 0% of the time, Pallas kernels for 0%

profile of v1, /device:TPU:0, one launch (start us, length us, event | category | flops | bytes accessed | tf_op | source)
XLA Modules:
  0.0 293.0 jit_solution(16287565726024425668)
XLA Ops:
  6.5 1.6 fusion.46
  8.2 2.3 all-gather
  10.9 11.7 %cholesky.50 = f32[128,128]{1,0:T(8,128)S(1)} custom-call(f32[128,128]{1,0:T(8,128)S(1)} %cholesky.118), custom_call_target="Cholesky" | custom-call | tf_op jit(solution)/shard_map/jit(cholesky)/cholesky | solution.py:29
  22.7 9.8 %custom-call.18 = f32[1,128,128]{1,2,0:T(8,128)S(1)} custom-call(f32[1,128,128]{2,1,0:T(8,128)S(1)} %get-tuple-element.28), custom_call_target="InvertDiagBlocksLowerTriangular" | custom-call | tf_op jit(solution)/shard_map/jit(cholesky)/cholesky | solution.py:29
  33.0 11.7 %cholesky.105 = f32[128,128]{1,0:T(8,128)S(1)} custom-call(f32[128,128]{1,0:T(8,128)S(1)} %convolution_subtract_fusion.2), custom_call_target="Cholesky" | custom-call | tf_op jit(solution)/shard_map/jit(cholesky)/cholesky | solution.py:29
  44.7 0.7 compare_reduce_fusion
  46.8 4.1 %while.1 = (s32[]{:T(128)}, f32[256,256]{1,0:T(8,128)S(1)}, s32[2,2]{1,0:T(2,128)S(1)}, f32[2,128,128]{2,1,0:T(8,128)S(1)}, s32[]{:T(128)}) while((s32[]{:T(128)}, f32[256,256]{1,0:T(8,128)S(1)}, s32[2,2]{1,0:T(2,128)S(1)}, f32[2,128,128]{2,1,0:T(8,128)S(1)}, s32[]{:T(128)}) %tuple.30), condition=%wide.while_cond, body=%wide.while_body.sunk | while | flops 2 | bytes 131181 | solution.py:30
  47.6 1.3 bitcast_dynamic-update-slice_fusion.2
  49.5 1.3 bitcast_dynamic-update-slice_fusion.2
  50.9 19.7 %custom-call.19 = f32[2,128,128]{1,2,0:T(8,128)S(1)} custom-call(f32[2,128,128]{2,1,0:T(8,128)S(1)} %get-tuple-element.12), custom_call_target="InvertDiagBlocksLowerTriangular" | custom-call | tf_op jit(solution)/shard_map/jit(_cho_solve)/triangular_solve | solution.py:30
  74.5 2.9 collective-permute-start
  77.4 27.5 %collective-permute-done = bf16[2,256,1024]{2,1,0:T(8,128)(2,1)S(1)} collective-permute-done((bf16[2,256,1024]{2,1,0:T(8,128)(2,1)S(1)}, bf16[2,256,1024]{2,1,0:T(8,128)(2,1)S(1)}, u32[]{:S(2)}, u32[]{:S(2)}) %collective-permute-start) | collective-permute-done | bytes 1048608 | tf_op jit(solution)/shard_map/ppermute | solution.py:10
  104.9 28.3 %collective-permute-done.1 = bf16[2,256,1024]{2,1,0:T(8,128)(2,1)} collective-permute-done((bf16[2,256,1024]{2,1,0:T(8,128)(2,1)S(1)}, bf16[2,256,1024]{2,1,0:T(8,128)(2,1)}, u32[]{:S(2)}, u32[]{:S(2)}) %collective-permute-start.1) | collective-permute-done | bytes 1048608 | tf_op jit(solution)/shard_map/ppermute | solution.py:10
  133.2 0.7 fusion.45
  135.8 25.1 %collective-permute-done.2 = bf16[2,256,1024]{2,1,0:T(8,128)(2,1)} collective-permute-done((bf16[2,256,1024]{2,1,0:T(8,128)(2,1)}, bf16[2,256,1024]{2,1,0:T(8,128)(2,1)}, u32[]{:S(2)}, u32[]{:S(2)}) %collective-permute-start.2) | collective-permute-done | bytes 1048608 | tf_op jit(solution)/shard_map/ppermute | solution.py:10
  160.9 1.9 pad_maximum_fusion
  162.8 1.9 copy-done.3
  164.8 3.2 %convolution_bitcast_fusion = f32[1024,256]{0,1:T(8,128)} fusion(f32[1024,1024]{1,0:T(8,128)S(1)} %copy-done.4, bf16[4,2,256,1024]{3,2,1,0:T(8,128)(2,1)S(1)} %pad_maximum_fusion, s32[]{:T(128)S(6)} %select_n.23), kind=kOutput, calls=%fused_computation.7 | convolution fusion | flops 3221225472 | bytes 5767172 | tf_op jit(solution)/shard_map/dot_general | solution.py:49
  174.0 9.4 %all-reduce.6.cloned.1.call-done = f32[1024,256]{0,1:T(8,128)} async-done(((f32[1024,256]{0,1:T(8,128)}), f32[1024,256]{0,1:T(8,128)}) %all-reduce.6.cloned.1.call-update) | async-done | bytes 1048592 | tf_op jit(solution)/shard_map/psum | solution.py:50
  183.5 4.9 %convolution_add_fusion.3 = f32[1024,1024]{1,0:T(8,128)S(1)} fusion(f32[1024,1024]{1,0:T(8,128)} %param.7, f32[32,8,8,128]{3,2,1,0:T(8,128)S(1)} %bitcast.128, f32[1024,256]{0,1:T(8,128)} %all-reduce.6.cloned.1.call-done, bf16[4,2,256,1024]{3,2,1,0:T(8,128)(2,1)} %copy-done.3, s32[]{:T(128)S(6)} %select_n.23, s32[]{:T(128)S(6)} %add.82), kind=kOutput, calls=%fused_computation.6 | convolution fusion | flops 3222798336 | bytes 11010056 | tf_op jit(solution)/shard_map/dot_general | solution.py:51
  188.4 2.0 copy-done.2
  190.5 4.2 %fusion.11 = f32[1024,256]{0,1:T(8,128)} fusion(f32[1024,1024]{1,0:T(8,128)S(1)} %convolution_add_fusion.3, bf16[4,2,256,1024]{3,2,1,0:T(8,128)(2,1)} %copy-done.3, s32[]{:T(128)S(6)} %select_n.24), kind=kOutput, calls=%fused_computation.34 | convolution fusion | flops 3221225472 | bytes 5767172 | tf_op jit(solution)/shard_map/dot_general | solution.py:49
  194.8 20.7 %all-reduce.8.cloned.1.call-done = f32[1024,256]{0,1:T(8,128)} async-done(((f32[1024,256]{0,1:T(8,128)}), f32[1024,256]{0,1:T(8,128)}) %all-reduce.8.cloned.1.call-update) | async-done | bytes 1048592 | tf_op jit(solution)/shard_map/psum | solution.py:50
  215.6 4.9 %convolution_add_fusion.2 = f32[1024,1024]{1,0:T(8,128)S(1)} fusion(f32[1024,1024]{1,0:T(8,128)} %copy-done.2, f32[32,8,8,128]{3,2,1,0:T(8,128)S(1)} %bitcast.126, f32[1024,256]{0,1:T(8,128)} %all-reduce.8.cloned.1.call-done, bf16[4,2,256,1024]{3,2,1,0:T(8,128)(2,1)} %copy-done.3, s32[]{:T(128)S(6)} %select_n.24, s32[]{:T(128)S(6)} %add.82), kind=kOutput, calls=%fused_computation.5 | convolution fusion | flops 3222798336 | bytes 11010056 | tf_op jit(solution)/shard_map/dot_general | solution.py:51
  220.5 2.0 copy-done.1
  222.5 4.2 %fusion.10 = f32[1024,256]{0,1:T(8,128)} fusion(f32[1024,1024]{1,0:T(8,128)S(1)} %convolution_add_fusion.2, bf16[4,2,256,1024]{3,2,1,0:T(8,128)(2,1)} %copy-done.3, s32[]{:T(128)S(6)} %select_n.25), kind=kOutput, calls=%fused_computation.31 | convolution fusion | flops 3221225472 | bytes 5767172 | tf_op jit(solution)/shard_map/dot_general | solution.py:49
  227.1 20.4 %all-reduce.10.cloned.1.call-done = f32[1024,256]{0,1:T(8,128)} async-done(((f32[1024,256]{0,1:T(8,128)}), f32[1024,256]{0,1:T(8,128)}) %all-reduce.10.cloned.1.call-update) | async-done | bytes 1048592 | tf_op jit(solution)/shard_map/psum | solution.py:50
  247.7 4.9 %convolution_add_fusion.1 = f32[1024,1024]{1,0:T(8,128)S(1)} fusion(f32[1024,1024]{1,0:T(8,128)} %copy-done.1, f32[32,8,8,128]{3,2,1,0:T(8,128)S(1)} %bitcast.127, f32[1024,256]{0,1:T(8,128)} %all-reduce.10.cloned.1.call-done, bf16[4,2,256,1024]{3,2,1,0:T(8,128)(2,1)} %copy-done.3, s32[]{:T(128)S(6)} %select_n.25, s32[]{:T(128)S(6)} %add.82), kind=kOutput, calls=%fused_computation.4 | convolution fusion | flops 3222798336 | bytes 11010056 | tf_op jit(solution)/shard_map/dot_general | solution.py:51
  252.6 2.0 copy-done
  254.6 4.2 %fusion.9 = f32[1024,256]{0,1:T(8,128)} fusion(f32[1024,1024]{1,0:T(8,128)S(1)} %convolution_add_fusion.1, bf16[4,2,256,1024]{3,2,1,0:T(8,128)(2,1)} %copy-done.3, s32[]{:T(128)S(6)} %select_n.26), kind=kOutput, calls=%fused_computation.28 | convolution fusion | flops 3221225472 | bytes 5767172 | tf_op jit(solution)/shard_map/dot_general | solution.py:49
  258.9 20.8 %all-reduce.12.cloned.1.call-done = f32[1024,256]{0,1:T(8,128)} async-done(((f32[1024,256]{0,1:T(8,128)}), f32[1024,256]{0,1:T(8,128)}) %all-reduce.12.cloned.1.call-update) | async-done | bytes 1048592 | tf_op jit(solution)/shard_map/psum | solution.py:50
  279.8 6.7 %convolution_add_fusion = f32[1024,1024]{1,0:T(8,128)} fusion(f32[1024,1024]{1,0:T(8,128)} %copy-done, f32[32,8,8,128]{3,2,1,0:T(8,128)S(1)} %bitcast.125, f32[1024,256]{0,1:T(8,128)} %all-reduce.12.cloned.1.call-done, bf16[4,2,256,1024]{3,2,1,0:T(8,128)(2,1)} %copy-done.3, s32[]{:T(128)S(6)} %select_n.26, s32[]{:T(128)S(6)} %add.82), kind=kOutput, calls=%fused_computation.3 | convolution fusion | flops 3222798336 | bytes 11010056 | tf_op jit(solution)/shard_map/dot_general | solution.py:51
  (62 shorter events, 7.5 us)
Async XLA Ops:
  6.5 64.1 %copy-start.6 = (f32[256,1024]{1,0:T(8,128)S(1)}, f32[256,1024]{1,0:T(8,128)}, u32[]{:S(2)}) copy-start(f32[256,1024]{1,0:T(8,128)} %param.9) | copy-start | bytes 3145732
  6.5 176.9 %all-reduce.6.cloned.1.call-start = ((), (), s32[]{:S(2)}) async-start(), calls=%async_computation | async-start | bytes 2097152 | tf_op jit(solution)/shard_map/psum | solution.py:50
  50.9 23.4 %copy-start.5 = (bf16[256,1024]{1,0:T(8,128)(2,1)S(1)}, bf16[256,1024]{1,0:T(8,128)(2,1)}, u32[]{:S(2)}) copy-start(bf16[256,1024]{1,0:T(8,128)(2,1)} %param.8) | copy-start | bytes 1572868
  71.8 61.4 %copy-start.9 = (s32[1,4]{1,0:T(1,128)S(1)}, s32[1,4]{1,0:T(1,128)}, u32[]{:S(2)}) copy-start(s32[1,4]{1,0:T(1,128)} %param.13) | copy-start | bytes 52
  74.5 30.4 %collective-permute-start = (bf16[2,256,1024]{2,1,0:T(8,128)(2,1)S(1)}, bf16[2,256,1024]{2,1,0:T(8,128)(2,1)S(1)}, u32[]{:S(2)}, u32[]{:S(2)}) collective-permute-start(bf16[2,256,1024]{2,1,0:T(8,128)(2,1)S(1)} %get-tuple-element.24), channel_id=1, source_target_pairs={{0,2},{2,4},{4,6},{6,8},{8,10},{10,12},{12,14},{14,16},{16,18},{18... | collective-permute-start | bytes 3145736 | tf_op jit(solution)/shard_map/ppermute | solution.py:10
  104.9 28.3 %collective-permute-start.1 = (bf16[2,256,1024]{2,1,0:T(8,128)(2,1)S(1)}, bf16[2,256,1024]{2,1,0:T(8,128)(2,1)}, u32[]{:S(2)}, u32[]{:S(2)}) collective-permute-start(bf16[2,256,1024]{2,1,0:T(8,128)(2,1)S(1)} %collective-permute-done), channel_id=1, source_target_pairs={{0,2},{2,4},{4,6},{6,8},{8,10},{10,12},{12,14},{14,16},{16,18},{18... | collective-permute-start | bytes 3145736 | tf_op jit(solution)/shard_map/ppermute | solution.py:10
  133.2 27.7 %collective-permute-start.2 = (bf16[2,256,1024]{2,1,0:T(8,128)(2,1)}, bf16[2,256,1024]{2,1,0:T(8,128)(2,1)}, u32[]{:S(2)}, u32[]{:S(2)}) collective-permute-start(bf16[2,256,1024]{2,1,0:T(8,128)(2,1)} %collective-permute-done.1), channel_id=1, source_target_pairs={{0,2},{2,4},{4,6},{6,8},{8,10},{10,12},{12,14},{14,16},{16,18},{18... | collective-permute-start | bytes 3145736 | tf_op jit(solution)/shard_map/ppermute | solution.py:10
  160.9 3.9 %copy-start.4 = (f32[1024,1024]{1,0:T(8,128)S(1)}, f32[1024,1024]{1,0:T(8,128)}, u32[]{:S(2)}) copy-start(f32[1024,1024]{1,0:T(8,128)} %param.7) | copy-start | bytes 12582916
  162.8 1.9 copy-start.3
  164.7 9.0 %copy-start.8 = (s32[1,4,8,4]{2,3,1,0:T(4,128)S(1)}, s32[1,4,8,4]{2,3,1,0:T(4,128)}, u32[]{:S(2)}) copy-start(s32[1,4,8,4]{2,3,1,0:T(4,128)} %param.11) | copy-start | bytes 1540
  164.7 9.0 %copy-start.10 = (f32[8]{0:T(128)S(1)}, f32[8]{0:T(128)}, u32[]{:S(2)}) copy-start(f32[8]{0:T(128)} %param.12) | copy-start | bytes 100
  164.7 9.2 %copy-start.7 = (s32[1,4,8,4]{2,3,1,0:T(4,128)S(1)}, s32[1,4,8,4]{2,3,1,0:T(4,128)}, u32[]{:S(2)}) copy-start(s32[1,4,8,4]{2,3,1,0:T(4,128)} %param.10) | copy-start | bytes 1540
  167.9 47.5 %all-reduce.8.cloned.1.call-start = ((), (), s32[]{:S(2)}) async-start(), calls=%async_computation.1 | async-start | bytes 2097152 | tf_op jit(solution)/shard_map/psum | solution.py:50
  188.4 2.0 copy-start.2
  194.7 52.8 %all-reduce.10.cloned.1.call-start = ((), (), s32[]{:S(2)}) async-start(), calls=%async_computation.2 | async-start | bytes 2097152 | tf_op jit(solution)/shard_map/psum | solution.py:50
  220.5 2.0 copy-start.1
  226.8 52.8 %all-reduce.12.cloned.1.call-start = ((), (), s32[]{:S(2)}) async-start(), calls=%async_computation.3 | async-start | bytes 2097152 | tf_op jit(solution)/shard_map/psum | solution.py:50
  252.6 2.0 copy-start
Sparse Core Ops, SparseCore 0:
  168.1 15.2 all-reduce.5
  194.8 20.5 all-reduce.7
  226.9 20.5 all-reduce.9
  259.0 20.5 all-reduce.11
